TPU v7x, 32 devices: a whole 2x2x4 slice. The times are simulated.
32 devices in a mesh: freq: 32 (over z, y, x, core).
Axes of the slice: x: 2, y: 2, z: 4, core: 2. Of those that a mesh axis runs over, the one named last changes fastest.
Arguments:
- model_vis: bfloat16 [64, 8, 4096], P('freq'), may hold values from -6 to 6
- observed: float32 [64, 4096], P('freq'), may hold values from -48 to 48
- row_keep: int32 [64, 4096], P('freq'), may hold values 0 or 1
- station_one: int32 [4096], replicated, may hold values from 0 to 61, as said below
- station_two: int32 [4096], replicated, may hold values from 0 to 61
- smoothness: float32 [496], replicated, may hold values from 4 to 24576
Outputs:
- gains: float32 [64, 496], P('freq')
Inputs may be any that keep to these rules, and one draw needn't show every extreme that they name: station_one and station_two differ in every row.
All inputs are finite; a program needn't handle non-finite values. No bound on the sum of `row_keep` on one device may be relied on, other than what follows from the above.
Results may differ from a plain program's by a relative error of at most 0.0003.
Values sent between devices are 32-bit elements; how exact they have to be, the bound alone decides.
A program may use at most 256 MiB of HBM per device.

v0:
```python
import jax
import jax.numpy as jnp
from jax import lax
from jax.sharding import PartitionSpec as P

STATIONS = 62
DIRECTIONS = 8


ridge_weight = 1.0


def from_behind(block, axis, distance):
    devices = range(lax.axis_size(axis))
    route = [(i - distance, i) for i in devices if i - distance in devices]
    return lax.ppermute(block, axis, route)


def product(left, right):
    return jnp.dot(left, right, precision=lax.Precision.HIGHEST)


def solve_with(factor, source):
    inner = jax.scipy.linalg.solve_triangular(factor, source, lower=True)
    return jax.scipy.linalg.solve_triangular(factor, inner, lower=True, trans=1)


def normal_system(model_channel, data_channel, keep_channel, station_one, station_two):
    coherence = model_channel.astype(jnp.float32).T
    weights = keep_channel.astype(jnp.float32)
    row_count = coherence.shape[0]
    outer_terms = (weights[:, None, None] * coherence[:, :, None] * coherence[:, None, :]).reshape(
        row_count, DIRECTIONS * DIRECTIONS
    )
    pair_one = station_one * STATIONS + station_two
    pair_two = station_two * STATIONS + station_one
    crossed = jax.ops.segment_sum(outer_terms, pair_one, STATIONS * STATIONS) + jax.ops.segment_sum(
        outer_terms, pair_two, STATIONS * STATIONS
    )
    selfed = jax.ops.segment_sum(outer_terms, station_one, STATIONS) + jax.ops.segment_sum(
        outer_terms, station_two, STATIONS
    )
    crossed = crossed.reshape(STATIONS, STATIONS, DIRECTIONS, DIRECTIONS)
    identity = jnp.eye(STATIONS, dtype=jnp.float32)
    blocks = crossed + identity[:, :, None, None] * selfed.reshape(
        STATIONS, 1, DIRECTIONS, DIRECTIONS
    )
    normal = blocks.transpose(2, 0, 3, 1).reshape(DIRECTIONS * STATIONS, DIRECTIONS * STATIONS)
    projected = (weights * data_channel)[:, None] * coherence
    target = jax.ops.segment_sum(projected, station_one, STATIONS) + jax.ops.segment_sum(
        projected, station_two, STATIONS
    )
    return (normal, target.T.reshape(DIRECTIONS * STATIONS))


def eliminate(reduced_diag, reduced_lower, reduced_upper, reduced_source):
    block_width = reduced_diag.shape[0]
    factor = jnp.linalg.cholesky(reduced_diag)
    solved = solve_with(
        factor, jnp.concatenate([reduced_lower, reduced_upper, reduced_source[:, None]], axis=1)
    )
    return (
        solved[:, :block_width],
        solved[:, block_width : 2 * block_width],
        solved[:, 2 * block_width],
    )


def body(model_vis, observed, row_keep, station_one, station_two, smoothness):
    channel_count = model_vis.shape[0]
    interior = channel_count - 1
    devices = lax.axis_size("freq")
    position = lax.axis_index("freq")
    block_width = smoothness.shape[0]
    last_channel = channel_count * devices - 1
    identity = jnp.eye(block_width, dtype=jnp.float32)
    left_scale = jnp.where(position > 0, smoothness, jnp.zeros_like(smoothness))

    def assemble(local_channel, model_channel, data_channel, keep_channel):
        normal, target = normal_system(
            model_channel, data_channel, keep_channel, station_one, station_two
        )
        global_channel = position * channel_count + local_channel
        neighbours = (
            2.0
            - (global_channel == 0).astype(jnp.float32)
            - (global_channel == last_channel).astype(jnp.float32)
        )
        return (normal + jnp.diag(ridge_weight + neighbours * smoothness), target)

    def forward(carried, channel_items):
        previous_inverse, previous_left, previous_right, previous_vector = carried
        local_channel, model_channel, data_channel, keep_channel = channel_items
        diagonal_block, target = assemble(local_channel, model_channel, data_channel, keep_channel)
        pivot_block = diagonal_block - smoothness[:, None] * previous_inverse * smoothness[None, :]
        source_left = (
            jnp.where(local_channel == 0, jnp.diag(left_scale), 0.0)
            + smoothness[:, None] * previous_left
        )
        source_right = (
            jnp.where(local_channel == interior - 1, jnp.diag(smoothness), 0.0)
            + smoothness[:, None] * previous_right
        )
        source_vector = target + smoothness * previous_vector
        factor = jnp.linalg.cholesky(pivot_block)
        inverse = solve_with(factor, identity)
        solved_left = product(inverse, source_left)
        solved_right = product(inverse, source_right)
        solved_vector = product(inverse, source_vector)
        return (
            (inverse, solved_left, solved_right, solved_vector),
            (inverse * smoothness[None, :], solved_left, solved_right, solved_vector),
        )

    zero_block = jnp.zeros((block_width, block_width), jnp.float32)
    zero_vector = jnp.zeros((block_width,), jnp.float32)
    local_channels = jnp.arange(interior, dtype=jnp.int32)
    finished, stacked = lax.scan(
        forward,
        (zero_block, zero_block, zero_block, zero_vector),
        (local_channels, model_vis[:interior], observed[:interior], row_keep[:interior]),
    )

    def backward(later, channel_items):
        later_left, later_right, later_vector = later
        coupling, solved_left, solved_right, solved_vector = channel_items
        current = (
            solved_left + product(coupling, later_left),
            solved_right + product(coupling, later_right),
            solved_vector + product(coupling, later_vector),
        )
        return (current, current)

    finished_back, columns = lax.scan(
        backward, (zero_block, zero_block, zero_vector), stacked, reverse=True
    )
    left_columns, right_columns, vector_columns = columns
    separator_block, separator_target = assemble(
        interior, model_vis[interior], observed[interior], row_keep[interior]
    )
    from_next = from_behind(
        (
            smoothness[:, None] * left_columns[0],
            smoothness[:, None] * right_columns[0],
            smoothness * vector_columns[0],
        ),
        "freq",
        -1,
    )
    reduced_diag = (
        separator_block - smoothness[:, None] * right_columns[interior - 1] - from_next[0]
    )
    reduced_lower = -smoothness[:, None] * left_columns[interior - 1]
    reduced_upper = -from_next[1]
    reduced_source = separator_target + smoothness * vector_columns[interior - 1] + from_next[2]
    levels = (devices - 1).bit_length()
    for level_index in range(levels):
        stride = 1 << level_index
        pieces = eliminate(reduced_diag, reduced_lower, reduced_upper, reduced_source)
        from_below = from_behind((pieces[0], pieces[1], pieces[2]), "freq", stride)
        from_above = from_behind((pieces[0], pieces[1], pieces[2]), "freq", -stride)
        reduced_diag, reduced_lower, reduced_upper, reduced_source = (
            reduced_diag
            - product(reduced_lower, from_below[1])
            - product(reduced_upper, from_above[0]),
            -product(reduced_lower, from_below[0]),
            -product(reduced_upper, from_above[1]),
            reduced_source
            - product(reduced_lower, from_below[2])
            - product(reduced_upper, from_above[2]),
        )
    separator = solve_with(jnp.linalg.cholesky(reduced_diag), reduced_source[:, None])[:, 0]
    earlier = from_behind(separator, "freq", 1)
    interior_gains = (
        vector_columns
        + jnp.einsum("mab,b->ma", left_columns, earlier, precision=lax.Precision.HIGHEST)
        + jnp.einsum("mab,b->ma", right_columns, separator, precision=lax.Precision.HIGHEST)
    )
    return jnp.concatenate([interior_gains, separator[None, :]], axis=0)


def solution(mesh):
    placed = (P("freq", None, None), P("freq", None), P("freq", None), P(), P(), P())
    return jax.shard_map(
        body, mesh=mesh, in_specs=placed, out_specs=P("freq", None), check_vma=False
    )
```

profile of v0, /device:TPU:8, one launch (start us, length us, event | category | flops | bytes accessed | tf_op | source)
XLA Modules:
  0.0 1918.5 jit_solution(16078973487524363337)
XLA Ops:
  8.3 22.4 %scatter_custom_fusion.4 = f32[62,8]{1,0:T(8,128)S(1)} fusion(s32[4096]{0:T(1024)S(1)} %copy-done.65, f32[4096,8]{1,0:T(8,128)S(1)} %copy.208, f32[]{:T(128)} %constant.258.clone.1), kind=kCustom, calls=%fused_computation.653 | custom fusion | flops 32768 | bytes 1988 | tf_op jit(solution)/shard_map/while/body/eval_jaxpr/scatter-add | solution.py:50
  30.7 22.4 %scatter_custom_fusion.5 = f32[62,8]{1,0:T(8,128)S(1)} fusion(s32[4096]{0:T(1024)S(1)} %copy-done.66, f32[4096,8]{1,0:T(8,128)S(1)} %copy.208, f32[]{:T(128)} %constant.258.clone.1), kind=kCustom, calls=%fused_computation.651 | custom fusion | flops 32768 | bytes 1988 | tf_op jit(solution)/shard_map/while/body/eval_jaxpr/scatter-add | solution.py:50
  56.8 23.1 %scatter_custom_fusion.6 = f32[3844,64]{1,0:T(8,128)S(1)} fusion(s32[4096]{0:T(1024)} %get-tuple-element.354, f32[4096,64]{1,0:T(8,128)} %copy.211, f32[]{:T(128)} %constant.258.clone.1), kind=kCustom, calls=%fused_computation.243 | custom fusion | flops 262144 | bytes 984576 | tf_op jit(solution)/shard_map/scatter-add | solution.py:37
  79.9 24.1 %scatter_custom_fusion.7 = f32[3844,64]{1,0:T(8,128)} fusion(s32[4096]{0:T(1024)} %get-tuple-element.353, f32[4096,64]{1,0:T(8,128)} %copy.211, f32[]{:T(128)} %constant.258.clone.1), kind=kCustom, calls=%fused_computation.241 | custom fusion | flops 262144 | bytes 984576 | tf_op jit(solution)/shard_map/scatter-add | solution.py:37
  113.6 22.7 %scatter_custom_fusion.8 = f32[62,64]{1,0:T(8,128)S(1)} fusion(s32[4096]{0:T(1024)} %param.14, f32[4096,64]{1,0:T(8,128)} %copy.211, f32[]{:T(128)} %constant.258.clone.1), kind=kCustom, calls=%fused_computation.657 | custom fusion | flops 262144 | bytes 16384 | tf_op jit(solution)/shard_map/scatter-add | solution.py:40
  136.2 22.7 %scatter_custom_fusion.9 = f32[62,64]{1,0:T(8,128)S(1)} fusion(s32[4096]{0:T(1024)} %param.15, f32[4096,64]{1,0:T(8,128)} %copy.211, f32[]{:T(128)} %constant.258.clone.1), kind=kCustom, calls=%fused_computation.655 | custom fusion | flops 262144 | bytes 16384 | tf_op jit(solution)/shard_map/scatter-add | solution.py:40
  161.0 23.1 %scatter_custom_fusion = f32[3844,64]{1,0:T(8,128)S(1)} fusion(s32[4096]{0:T(1024)} %get-tuple-element.354, f32[4096,64]{1,0:T(8,128)} %copy.186, f32[]{:T(128)} %constant.258.clone.1), kind=kCustom, calls=%fused_computation.247 | custom fusion | flops 262144 | bytes 984576 | tf_op jit(solution)/shard_map/while/body/eval_jaxpr/scatter-add | solution.py:37
  184.1 24.2 %scatter_custom_fusion.1 = f32[3844,64]{1,0:T(8,128)} fusion(s32[4096]{0:T(1024)} %get-tuple-element.353, f32[4096,64]{1,0:T(8,128)} %copy.186, f32[]{:T(128)} %constant.258.clone.1), kind=kCustom, calls=%fused_computation.245 | custom fusion | flops 262144 | bytes 984576 | tf_op jit(solution)/shard_map/while/body/eval_jaxpr/scatter-add | solution.py:37
  217.8 22.7 %scatter_custom_fusion.2 = f32[62,64]{1,0:T(8,128)S(1)} fusion(s32[4096]{0:T(1024)} %param.14, f32[4096,64]{1,0:T(8,128)} %copy.186, f32[]{:T(128)} %constant.258.clone.1), kind=kCustom, calls=%fused_computation.661 | custom fusion | flops 262144 | bytes 16384 | tf_op jit(solution)/shard_map/while/body/eval_jaxpr/scatter-add | solution.py:40
  240.5 22.7 %scatter_custom_fusion.3 = f32[62,64]{1,0:T(8,128)S(1)} fusion(s32[4096]{0:T(1024)} %param.15, f32[4096,64]{1,0:T(8,128)} %copy.186, f32[]{:T(128)} %constant.258.clone.1), kind=kCustom, calls=%fused_computation.659 | custom fusion | flops 262144 | bytes 16384 | tf_op jit(solution)/shard_map/while/body/eval_jaxpr/scatter-add | solution.py:40
  277.9 11.7 cholesky.752
  303.0 12.5 cholesky.771
  328.8 11.7 cholesky.792
  377.7 39.5 %custom-call.41 = f32[4,128,128]{1,2,0:T(8,128)S(1)} custom-call(f32[4,128,128]{2,1,0:T(8,128)S(1)} %pad_maximum_fusion.11), custom_call_target="InvertDiagBlocksLowerTriangular" | custom-call | tf_op jit(solution)/shard_map/while/body/eval_jaxpr/jit(_solve_triangular)/triangular_solve | solution.py:25
  458.4 22.7 %scatter_custom_fusion.10 = f32[62,8]{1,0:T(8,128)S(1)} fusion(s32[4096]{0:T(1024)} %param.14, f32[4096,8]{1,0:T(8,128)} %copy.226, f32[]{:T(128)} %constant.258.clone.1), kind=kCustom, calls=%fused_computation.649 | custom fusion | flops 32768 | bytes 2496 | tf_op jit(solution)/shard_map/scatter-add | solution.py:50
  481.0 22.7 %scatter_custom_fusion.11 = f32[62,8]{1,0:T(8,128)S(1)} fusion(s32[4096]{0:T(1024)} %param.15, f32[4096,8]{1,0:T(8,128)} %copy.226, f32[]{:T(128)} %constant.258.clone.1), kind=kCustom, calls=%fused_computation.647 | custom fusion | flops 32768 | bytes 2496 | tf_op jit(solution)/shard_map/scatter-add | solution.py:50
  521.8 11.7 cholesky.828
  548.6 11.7 cholesky.847
  574.8 11.7 cholesky.868
  630.2 40.9 %custom-call.76 = f32[4,128,128]{1,2,0:T(8,128)} custom-call(f32[4,128,128]{2,1,0:T(8,128)} %pad_maximum_fusion.12), custom_call_target="InvertDiagBlocksLowerTriangular" | custom-call | tf_op jit(solution)/shard_map/jit(_solve_triangular)/triangular_solve | solution.py:25
  723.1 14.3 collective-permute-done.3
  742.5 11.7 cholesky.904
  767.2 11.7 cholesky.923
  790.6 11.7 cholesky.944
  839.8 40.3 %custom-call.81 = f32[4,128,128]{1,2,0:T(8,128)} custom-call(f32[4,128,128]{2,1,0:T(8,128)S(1)} %pad_maximum_fusion.13), custom_call_target="InvertDiagBlocksLowerTriangular" | custom-call | tf_op jit(solution)/shard_map/jit(_solve_triangular)/triangular_solve | solution.py:25
  911.2 12.4 collective-permute-start.10
  937.1 11.8 collective-permute-done.14
  959.1 52.7 %collective-permute-done.9 = f32[496,496]{0,1:T(8,128)} collective-permute-done((f32[496,496]{0,1:T(8,128)}, f32[496,496]{0,1:T(8,128)}, u32[]{:S(2)}, u32[]{:S(2)}) %collective-permute-start.9) | collective-permute-done | bytes 984096 | tf_op jit(solution)/shard_map/ppermute | solution.py:16
  1020.9 11.7 cholesky.980
  1046.5 11.7 cholesky.999
  1072.9 13.2 cholesky.1020
  1127.9 40.1 %custom-call.86 = f32[4,128,128]{1,2,0:T(8,128)} custom-call(f32[4,128,128]{2,1,0:T(8,128)S(1)} %pad_maximum_fusion.14), custom_call_target="InvertDiagBlocksLowerTriangular" | custom-call | tf_op jit(solution)/shard_map/jit(_solve_triangular)/triangular_solve | solution.py:25
  1217.7 33.2 %collective-permute-done.20 = f32[496]{0:T(512)S(1)} collective-permute-done((f32[496]{0:T(512)S(1)}, f32[496]{0:T(512)S(1)}, u32[]{:S(2)}, u32[]{:S(2)}) %collective-permute-start.20) | collective-permute-done | bytes 2016 | tf_op jit(solution)/shard_map/ppermute | solution.py:16
  1258.2 27.8 %collective-permute-done.15 = f32[496,496]{0,1:T(8,128)} collective-permute-done((f32[496,496]{0,1:T(8,128)}, f32[496,496]{0,1:T(8,128)}, u32[]{:S(2)}, u32[]{:S(2)}) %collective-permute-start.15) | collective-permute-done | bytes 984096 | tf_op jit(solution)/shard_map/ppermute | solution.py:16
  1295.1 11.7 cholesky.1056
  1320.5 11.7 cholesky.1075
  1346.8 13.2 cholesky.1096
  1402.1 40.1 %custom-call.91 = f32[4,128,128]{1,2,0:T(8,128)} custom-call(f32[4,128,128]{2,1,0:T(8,128)S(1)} %pad_maximum_fusion.15), custom_call_target="InvertDiagBlocksLowerTriangular" | custom-call | tf_op jit(solution)/shard_map/jit(_solve_triangular)/triangular_solve | solution.py:25
  1494.8 12.0 collective-permute-done.26
  1516.3 19.2 %collective-permute-done.21 = f32[496,496]{0,1:T(8,128)} collective-permute-done((f32[496,496]{0,1:T(8,128)}, f32[496,496]{0,1:T(8,128)}, u32[]{:S(2)}, u32[]{:S(2)}) %collective-permute-start.21) | collective-permute-done | bytes 984096 | tf_op jit(solution)/shard_map/ppermute | solution.py:16
  1570.0 11.7 cholesky.1151
  1596.3 13.2 cholesky.1172
  1651.4 40.3 %custom-call.96 = f32[4,128,128]{1,2,0:T(8,128)} custom-call(f32[4,128,128]{2,1,0:T(8,128)S(1)} %pad_maximum_fusion.16), custom_call_target="InvertDiagBlocksLowerTriangular" | custom-call | tf_op jit(solution)/shard_map/jit(_solve_triangular)/triangular_solve | solution.py:25
  1732.2 16.0 collective-permute-done.30
  1752.0 21.3 %collective-permute-done.27 = f32[496,496]{0,1:T(8,128)S(1)} collective-permute-done((f32[496,496]{0,1:T(8,128)S(1)}, f32[496,496]{0,1:T(8,128)S(1)}, u32[]{:S(2)}, u32[]{:S(2)}) %collective-permute-start.27) | collective-permute-done | bytes 984096 | tf_op jit(solution)/shard_map/ppermute | solution.py:16
  1799.0 11.7 cholesky.1227
  1821.5 11.7 cholesky.1248
  1866.0 40.1 %custom-call.42 = f32[4,128,128]{1,2,0:T(8,128)S(1)} custom-call(f32[4,128,128]{2,1,0:T(8,128)} %pad_maximum_fusion.17), custom_call_target="InvertDiagBlocksLowerTriangular" | custom-call | tf_op jit(solution)/shard_map/jit(_solve_triangular)/triangular_solve | solution.py:25
  (721 shorter events, 952.1 us)
Async XLA Ops:
  213.4 49.8 %copy-start.63 = (f32[62,62]{1,0:T(8,128)S(1)}, f32[62,62]{1,0:T(8,128)}, u32[]{:S(2)}) copy-start(f32[62,62]{1,0:T(8,128)} %fusion.412) | copy-start | bytes 46132
  327.4 40.1 %copy-start.70 = (pred[16,16]{1,0:T(8,128)(4,1)S(1)}, pred[16,16]{1,0:T(8,128)(4,1)}, u32[]{:S(2)}) copy-start(pred[16,16]{1,0:T(8,128)(4,1)} %iota_compare_fusion.9) | copy-start | bytes 772
  442.0 9.7 copy-start.44
  447.1 63.7 %collective-permute-start = (f32[496,496]{1,0:T(8,128)}, f32[496,496]{1,0:T(8,128)}, u32[]{:S(2)}, u32[]{:S(2)}) collective-permute-start(f32[496,496]{1,0:T(8,128)} %get-tuple-element.270), channel_id=1, source_target_pairs={{1,0},{2,1},{3,2},{4,3},{5,4},{6,5},{7,6},{8,7},{9,8},{10,9},{11,1... | collective-permute-start | bytes 2952200 | tf_op jit(solution)/shard_map/ppermute | solution.py:16
  453.4 55.8 %collective-permute-start.2 = (f32[496]{0:T(512)}, f32[496]{0:T(512)}, u32[]{:S(2)}, u32[]{:S(2)}) collective-permute-start(f32[496]{0:T(512)} %get-tuple-element.243), channel_id=1, source_target_pairs={{1,0},{2,1},{3,2},{4,3},{5,4},{6,5},{7,6},{8,7},{9,8},{10,9},{11,1... | collective-permute-start | bytes 5960 | tf_op jit(solution)/shard_map/ppermute | solution.py:16
  515.9 155.2 %collective-permute-start.1 = (f32[496,496]{1,0:T(8,128)}, f32[496,496]{1,0:T(8,128)S(1)}, u32[]{:S(2)}, u32[]{:S(2)}) collective-permute-start(f32[496,496]{1,0:T(8,128)} %get-tuple-element.242), channel_id=1, source_target_pairs={{1,0},{2,1},{3,2},{4,3},{5,4},{6,5},{7,6},{8,7},{9,8},{10,9},{11,1... | collective-permute-start | bytes 2952200 | tf_op jit(solution)/shard_map/ppermute | solution.py:16
  616.7 54.5 %copy-start.45 = (f32[496,1]{1,0:T(8,128)S(1)}, f32[496,1]{1,0:T(8,128)}, u32[]{:S(2)}) copy-start(f32[496,1]{1,0:T(8,128)} %copy.229) | copy-start | bytes 5956
  671.1 49.0 %copy-start.12 = (f32[496,496]{1,0:T(8,128)}, f32[496,496]{1,0:T(8,128)S(1)}, u32[]{:S(2)}) copy-start(f32[496,496]{1,0:T(8,128)S(1)} %collective-permute-done.1) | copy-start | bytes 2952196
  698.6 21.4 %collective-permute-start.4 = (f32[496,496]{0,1:T(8,128)}, f32[496,496]{0,1:T(8,128)}, u32[]{:S(2)}, u32[]{:S(2)}) collective-permute-start(f32[496,496]{0,1:T(8,128)} %get-tuple-element.267), channel_id=1, source_target_pairs={{1,0},{2,1},{3,2},{4,3},{5,4},{6,5},{7,6},{8,7},{9,8},{10,9},{11,1... | collective-permute-start | bytes 2952200 | tf_op jit(solution)/shard_map/ppermute | solution.py:16
  701.2 14.8 collective-permute-start.7
  703.1 15.7 collective-permute-start.8
  708.5 174.7 %collective-permute-start.5 = (f32[496,496]{0,1:T(8,128)}, f32[496,496]{0,1:T(8,128)}, u32[]{:S(2)}, u32[]{:S(2)}) collective-permute-start(f32[496,496]{0,1:T(8,128)} %get-tuple-element.267), channel_id=1, source_target_pairs={{0,1},{1,2},{2,3},{3,4},{4,5},{5,6},{6,7},{7,8},{8,9},{9,10},{10,1... | collective-permute-start | bytes 2952200 | tf_op jit(solution)/shard_map/ppermute | solution.py:16
  710.5 169.7 %collective-permute-start.6 = (f32[496,496]{0,1:T(8,128)}, f32[496,496]{0,1:T(8,128)}, u32[]{:S(2)}, u32[]{:S(2)}) collective-permute-start(f32[496,496]{0,1:T(8,128)} %get-tuple-element.268), channel_id=1, source_target_pairs={{1,0},{2,1},{3,2},{4,3},{5,4},{6,5},{7,6},{8,7},{9,8},{10,9},{11,1... | collective-permute-start | bytes 2952200 | tf_op jit(solution)/shard_map/ppermute | solution.py:16
  715.9 21.5 %collective-permute-start.3 = (f32[496,496]{0,1:T(8,128)}, f32[496,496]{0,1:T(8,128)}, u32[]{:S(2)}, u32[]{:S(2)}) collective-permute-start(f32[496,496]{0,1:T(8,128)} %get-tuple-element.268), channel_id=1, source_target_pairs={{0,1},{1,2},{2,3},{3,4},{4,5},{5,6},{6,7},{7,8},{8,9},{9,10},{10,1... | collective-permute-start | bytes 2952200 | tf_op jit(solution)/shard_map/ppermute | solution.py:16
  813.9 66.3 %copy-start.13 = (f32[496,496]{1,0:T(8,128)S(1)}, f32[496,496]{1,0:T(8,128)}, u32[]{:S(2)}) copy-start(f32[496,496]{1,0:T(8,128)} %copy-done.12) | copy-start | bytes 2952196
  911.2 44.9 %collective-permute-start.10 = (f32[496,496]{0,1:T(8,128)}, f32[496,496]{0,1:T(8,128)}, u32[]{:S(2)}, u32[]{:S(2)}) collective-permute-start(f32[496,496]{0,1:T(8,128)} %get-tuple-element.265), channel_id=1, source_target_pairs={{2,0},{3,1},{4,2},{5,3},{6,4},{7,5},{8,6},{9,7},{10,8},{11,9},{12,... | collective-permute-start | bytes 2952200 | tf_op jit(solution)/shard_map/ppermute | solution.py:16
  923.6 25.3 %collective-permute-start.14 = (f32[496]{0:T(512)S(1)}, f32[496]{0:T(512)S(1)}, u32[]{:S(2)}, u32[]{:S(2)}) collective-permute-start(f32[496]{0:T(512)S(1)} %bitcast.685), channel_id=1, source_target_pairs={{2,0},{3,1},{4,2},{5,3},{6,4},{7,5},{8,6},{9,7},{10,8},{11,9},{12,... | collective-permute-start | bytes 5960 | tf_op jit(solution)/shard_map/ppermute | solution.py:16
  925.5 29.4 %collective-permute-start.13 = (f32[496]{0:T(512)S(1)}, f32[496]{0:T(512)S(1)}, u32[]{:S(2)}, u32[]{:S(2)}) collective-permute-start(f32[496]{0:T(512)S(1)} %bitcast.686), channel_id=1, source_target_pairs={{0,2},{1,3},{2,4},{3,5},{4,6},{5,7},{6,8},{7,9},{8,10},{9,11},{10,... | collective-permute-start | bytes 5960 | tf_op jit(solution)/shard_map/ppermute | solution.py:16
  929.5 241.6 %collective-permute-start.11 = (f32[496,496]{0,1:T(8,128)}, f32[496,496]{0,1:T(8,128)}, u32[]{:S(2)}, u32[]{:S(2)}) collective-permute-start(f32[496,496]{0,1:T(8,128)} %get-tuple-element.265), channel_id=1, source_target_pairs={{0,2},{1,3},{2,4},{3,5},{4,6},{5,7},{6,8},{7,9},{8,10},{9,11},{10,... | collective-permute-start | bytes 2952200 | tf_op jit(solution)/shard_map/ppermute | solution.py:16
  934.0 234.0 %collective-permute-start.12 = (f32[496,496]{0,1:T(8,128)}, f32[496,496]{0,1:T(8,128)}, u32[]{:S(2)}, u32[]{:S(2)}) collective-permute-start(f32[496,496]{0,1:T(8,128)} %get-tuple-element.266), channel_id=1, source_target_pairs={{2,0},{3,1},{4,2},{5,3},{6,4},{7,5},{8,6},{9,7},{10,8},{11,9},{12,... | collective-permute-start | bytes 2952200 | tf_op jit(solution)/shard_map/ppermute | solution.py:16
  948.9 62.9 %collective-permute-start.9 = (f32[496,496]{0,1:T(8,128)}, f32[496,496]{0,1:T(8,128)}, u32[]{:S(2)}, u32[]{:S(2)}) collective-permute-start(f32[496,496]{0,1:T(8,128)} %get-tuple-element.266), channel_id=1, source_target_pairs={{0,2},{1,3},{2,4},{3,5},{4,6},{5,7},{6,8},{7,9},{8,10},{9,11},{10,... | collective-permute-start | bytes 2952200 | tf_op jit(solution)/shard_map/ppermute | solution.py:16
  954.9 56.9 %copy-start.5 = (f32[496,496]{1,0:T(8,128)S(1)}, f32[496,496]{1,0:T(8,128)}, u32[]{:S(2)}) copy-start(f32[496,496]{1,0:T(8,128)} %copy-done.4) | copy-start | bytes 2952196
  1171.1 13.7 copy-start
  1200.5 52.5 %copy-start.1 = (f32[496,496]{1,0:T(8,128)S(1)}, f32[496,496]{1,0:T(8,128)}, u32[]{:S(2)}) copy-start(f32[496,496]{1,0:T(8,128)} %copy-done) | copy-start | bytes 2952196
  1200.5 54.6 %collective-permute-start.16 = (f32[496,496]{0,1:T(8,128)}, f32[496,496]{0,1:T(8,128)}, u32[]{:S(2)}, u32[]{:S(2)}) collective-permute-start(f32[496,496]{0,1:T(8,128)} %get-tuple-element.263), channel_id=1, source_target_pairs={{4,0},{5,1},{6,2},{7,3},{8,4},{9,5},{10,6},{11,7},{12,8},{13,9},{1... | collective-permute-start | bytes 2952200 | tf_op jit(solution)/shard_map/ppermute | solution.py:16
  1205.1 45.8 %collective-permute-start.20 = (f32[496]{0:T(512)S(1)}, f32[496]{0:T(512)S(1)}, u32[]{:S(2)}, u32[]{:S(2)}) collective-permute-start(f32[496]{0:T(512)S(1)} %bitcast.687), channel_id=1, source_target_pairs={{4,0},{5,1},{6,2},{7,3},{8,4},{9,5},{10,6},{11,7},{12,8},{13,9},{1... | collective-permute-start | bytes 5960 | tf_op jit(solution)/shard_map/ppermute | solution.py:16
  1207.0 47.0 %collective-permute-start.19 = (f32[496]{0:T(512)S(1)}, f32[496]{0:T(512)S(1)}, u32[]{:S(2)}, u32[]{:S(2)}) collective-permute-start(f32[496]{0:T(512)S(1)} %bitcast.688), channel_id=1, source_target_pairs={{0,4},{1,5},{2,6},{3,7},{4,8},{5,9},{6,10},{7,11},{8,12},{9,13},{1... | collective-permute-start | bytes 5960 | tf_op jit(solution)/shard_map/ppermute | solution.py:16
  1210.9 234.3 %collective-permute-start.17 = (f32[496,496]{0,1:T(8,128)}, f32[496,496]{0,1:T(8,128)}, u32[]{:S(2)}, u32[]{:S(2)}) collective-permute-start(f32[496,496]{0,1:T(8,128)} %get-tuple-element.263), channel_id=1, source_target_pairs={{0,4},{1,5},{2,6},{3,7},{4,8},{5,9},{6,10},{7,11},{8,12},{9,13},{1... | collective-permute-start | bytes 2952200 | tf_op jit(solution)/shard_map/ppermute | solution.py:16
  1214.2 228.0 %collective-permute-start.18 = (f32[496,496]{0,1:T(8,128)}, f32[496,496]{0,1:T(8,128)}, u32[]{:S(2)}, u32[]{:S(2)}) collective-permute-start(f32[496,496]{0,1:T(8,128)} %get-tuple-element.264), channel_id=1, source_target_pairs={{4,0},{5,1},{6,2},{7,3},{8,4},{9,5},{10,6},{11,7},{12,8},{13,9},{1... | collective-permute-start | bytes 2952200 | tf_op jit(solution)/shard_map/ppermute | solution.py:16
  1250.9 35.0 %collective-permute-start.15 = (f32[496,496]{0,1:T(8,128)}, f32[496,496]{0,1:T(8,128)}, u32[]{:S(2)}, u32[]{:S(2)}) collective-permute-start(f32[496,496]{0,1:T(8,128)} %get-tuple-element.264), channel_id=1, source_target_pairs={{0,4},{1,5},{2,6},{3,7},{4,8},{5,9},{6,10},{7,11},{8,12},{9,13},{1... | collective-permute-start | bytes 2952200 | tf_op jit(solution)/shard_map/ppermute | solution.py:16
  1254.0 32.0 %copy-start.7 = (f32[496,496]{1,0:T(8,128)S(1)}, f32[496,496]{1,0:T(8,128)}, u32[]{:S(2)}) copy-start(f32[496,496]{1,0:T(8,128)} %fusion.63) | copy-start | bytes 2952196
  1473.2 40.0 %collective-permute-start.22 = (f32[496,496]{0,1:T(8,128)}, f32[496,496]{0,1:T(8,128)}, u32[]{:S(2)}, u32[]{:S(2)}) collective-permute-start(f32[496,496]{0,1:T(8,128)} %get-tuple-element.261), channel_id=1, source_target_pairs={{8,0},{9,1},{10,2},{11,3},{12,4},{13,5},{14,6},{15,7},{16,8},{17,9... | collective-permute-start | bytes 2952200 | tf_op jit(solution)/shard_map/ppermute | solution.py:16
  1482.1 24.7 %collective-permute-start.26 = (f32[496]{0:T(512)S(1)}, f32[496]{0:T(512)S(1)}, u32[]{:S(2)}, u32[]{:S(2)}) collective-permute-start(f32[496]{0:T(512)S(1)} %bitcast.689), channel_id=1, source_target_pairs={{8,0},{9,1},{10,2},{11,3},{12,4},{13,5},{14,6},{15,7},{16,8},{17,9... | collective-permute-start | bytes 5960 | tf_op jit(solution)/shard_map/ppermute | solution.py:16
  1484.0 28.1 %collective-permute-start.25 = (f32[496]{0:T(512)S(1)}, f32[496]{0:T(512)S(1)}, u32[]{:S(2)}, u32[]{:S(2)}) collective-permute-start(f32[496]{0:T(512)S(1)} %bitcast.690), channel_id=1, source_target_pairs={{0,8},{1,9},{2,10},{3,11},{4,12},{5,13},{6,14},{7,15},{8,16},{9,17... | collective-permute-start | bytes 5960 | tf_op jit(solution)/shard_map/ppermute | solution.py:16
  1487.9 206.8 %collective-permute-start.23 = (f32[496,496]{0,1:T(8,128)}, f32[496,496]{0,1:T(8,128)}, u32[]{:S(2)}, u32[]{:S(2)}) collective-permute-start(f32[496,496]{0,1:T(8,128)} %get-tuple-element.261), channel_id=1, source_target_pairs={{0,8},{1,9},{2,10},{3,11},{4,12},{5,13},{6,14},{7,15},{8,16},{9,17... | collective-permute-start | bytes 2952200 | tf_op jit(solution)/shard_map/ppermute | solution.py:16
  1491.3 200.4 %collective-permute-start.24 = (f32[496,496]{0,1:T(8,128)}, f32[496,496]{0,1:T(8,128)}, u32[]{:S(2)}, u32[]{:S(2)}) collective-permute-start(f32[496,496]{0,1:T(8,128)} %get-tuple-element.262), channel_id=1, source_target_pairs={{8,0},{9,1},{10,2},{11,3},{12,4},{13,5},{14,6},{15,7},{16,8},{17,9... | collective-permute-start | bytes 2952200 | tf_op jit(solution)/shard_map/ppermute | solution.py:16
  1506.8 28.7 %collective-permute-start.21 = (f32[496,496]{0,1:T(8,128)}, f32[496,496]{0,1:T(8,128)}, u32[]{:S(2)}, u32[]{:S(2)}) collective-permute-start(f32[496,496]{0,1:T(8,128)} %get-tuple-element.262), channel_id=1, source_target_pairs={{0,8},{1,9},{2,10},{3,11},{4,12},{5,13},{6,14},{7,15},{8,16},{9,17... | collective-permute-start | bytes 2952200 | tf_op jit(solution)/shard_map/ppermute | solution.py:16
  1512.1 23.4 %copy-start.9 = (f32[496,496]{1,0:T(8,128)S(1)}, f32[496,496]{1,0:T(8,128)}, u32[]{:S(2)}) copy-start(f32[496,496]{1,0:T(8,128)} %fusion.62) | copy-start | bytes 2952196
  1694.8 13.5 copy-start.2
  1722.4 25.8 %copy-start.3 = (f32[496,496]{1,0:T(8,128)S(1)}, f32[496,496]{1,0:T(8,128)}, u32[]{:S(2)}) copy-start(f32[496,496]{1,0:T(8,128)} %copy-done.2) | copy-start | bytes 2952196
  1722.4 27.8 %collective-permute-start.28 = (f32[496,496]{0,1:T(8,128)S(1)}, f32[496,496]{0,1:T(8,128)S(1)}, u32[]{:S(2)}, u32[]{:S(2)}) collective-permute-start(f32[496,496]{0,1:T(8,128)S(1)} %get-tuple-element.260), channel_id=1, source_target_pairs={{16,0},{17,1},{18,2},{19,3},{20,4},{21,5},{22,6},{23,7},{24,8},{25... | collective-permute-start | bytes 2952200 | tf_op jit(solution)/shard_map/ppermute | solution.py:16
  1723.8 24.4 %collective-permute-start.30 = (f32[496]{0:T(512)S(1)}, f32[496]{0:T(512)S(1)}, u32[]{:S(2)}, u32[]{:S(2)}) collective-permute-start(f32[496]{0:T(512)S(1)} %bitcast.699), channel_id=1, source_target_pairs={{16,0},{17,1},{18,2},{19,3},{20,4},{21,5},{22,6},{23,7},{24,8},{25... | collective-permute-start | bytes 5960 | tf_op jit(solution)/shard_map/ppermute | solution.py:16
  1725.1 24.0 %collective-permute-start.29 = (f32[496]{0:T(512)S(1)}, f32[496]{0:T(512)S(1)}, u32[]{:S(2)}, u32[]{:S(2)}) collective-permute-start(f32[496]{0:T(512)S(1)} %bitcast.700), channel_id=1, source_target_pairs={{0,16},{1,17},{2,18},{3,19},{4,20},{5,21},{6,22},{7,23},{8,24},{9,... | collective-permute-start | bytes 5960 | tf_op jit(solution)/shard_map/ppermute | solution.py:16
  1730.6 42.7 %collective-permute-start.27 = (f32[496,496]{0,1:T(8,128)S(1)}, f32[496,496]{0,1:T(8,128)S(1)}, u32[]{:S(2)}, u32[]{:S(2)}) collective-permute-start(f32[496,496]{0,1:T(8,128)S(1)} %get-tuple-element.259), channel_id=1, source_target_pairs={{0,16},{1,17},{2,18},{3,19},{4,20},{5,21},{6,22},{7,23},{8,24},{9,... | collective-permute-start | bytes 2952200 | tf_op jit(solution)/shard_map/ppermute | solution.py:16
  1749.1 24.2 %copy-start.11 = (f32[496,496]{1,0:T(8,128)S(1)}, f32[496,496]{1,0:T(8,128)}, u32[]{:S(2)}) copy-start(f32[496,496]{1,0:T(8,128)} %fusion.61) | copy-start | bytes 2952196
  1859.4 49.7 %copy-start.34 = (f32[496,496]{1,0:T(8,128)S(1)}, f32[496,496]{1,0:T(8,128)}, u32[]{:S(2)}) copy-start(f32[496,496]{1,0:T(8,128)} %get-tuple-element.364) | copy-start | bytes 2952196
  1859.4 57.4 %copy-start.33 = (f32[496,496]{1,0:T(8,128)S(1)}, f32[496,496]{1,0:T(8,128)}, u32[]{:S(2)}) copy-start(f32[496,496]{1,0:T(8,128)} %get-tuple-element.363) | copy-start | bytes 2952196
  1910.0 6.7 collective-permute-start.31
  (56 other events, 175.2 us)
where the time goes:
time: 1930 us; the launch traced here: 1920 us
  other arithmetic  1160 us (60%)
  matrix products  260 us (13%)
  waiting for transfers between devices  213 us (11%)
  local copies, waits for them, and re-layouts  149 us (8%)
  starting transfers between devices  116 us (6%)
  between operations  21.3 us (1%)
    another operation x75, other arithmetic, eliminate(): factor = jnp.linalg.cholesky(reduced_diag)  405 us
    another operation x37, other arithmetic, solve_with(): return jax.scipy.linalg.solve_triangular(factor, inner, lower=True, trans=1)  293 us
    ppermute x32, waiting for transfers between devices, from_behind(): return lax.ppermute(block, axis, route)  213 us
    ppermute x32, starting transfers between devices, from_behind(): return lax.ppermute(block, axis, route)  116 us
    another operation x15, other arithmetic, forward(): factor = jnp.linalg.cholesky(pivot_block)  80 us
    another operation x15, other arithmetic, body(): jnp.linalg.cholesky(reduced_diag)  77.7 us
    dot_general x33, matrix products, product(): return jnp.dot(left, right, precision=lax.Precision.HIGHEST)  77.5 us
    another operation x49, matrix products, solve_with(): return jax.scipy.linalg.solve_triangular(factor, inner, lower=True, trans=1)  68.4 us
  transfers between devices with their start and end apart: 32, of which 10 were waited for; matrix products, arithmetic and copies ran while one was open for 44% of the time, Pallas kernels for 0%

commit v1 on v0

v1 whole, which is shorter than its diff:
```python
import jax
import jax.numpy as jnp
from jax import lax
from jax.experimental import pallas as pl
from jax.experimental.pallas import tpu as pltpu
from jax.sharding import PartitionSpec as P

ridge_weight = 1.0
PANEL = 128
GROUP = 16
HIGHEST = lax.Precision.HIGHEST


def mm(left, right, dims=((1,), (0,))):
    return lax.dot_general(
        left, right, (dims, ((), ())), precision=HIGHEST, preferred_element_type=jnp.float32
    )


NT = ((1,), (1,))
TN = ((0,), (0,))


def invert_panel(block):
    size = block.shape[0]
    lane = lax.broadcasted_iota(jnp.int32, (1, size), 1)
    sub = lax.broadcasted_iota(jnp.int32, (size, 1), 0)

    def group(_, a):
        for k in range(GROUP):
            row = a[k : k + 1, :]
            col = a[:, k : k + 1]
            inv = 1.0 / a[k : k + 1, k : k + 1]
            scaled = jnp.where(lane == k, 1.0, row) * inv
            factor = jnp.where(sub == k, -1.0, col)
            rest = jnp.where((lane == k) | (sub == k), 0.0, a)
            a = rest - factor * scaled
        a = jnp.concatenate([a[GROUP:, :], a[:GROUP, :]], axis=0)
        return pltpu.roll(a, size - GROUP, 1)

    return lax.fori_loop(0, size // GROUP, group, block)


def invert_in_place(a_ref, row_ref):
    width = a_ref.shape[0]

    @pl.loop(0, width // PANEL)
    def _(step):
        own = pl.ds(pl.multiple_of(step * PANEL, PANEL), PANEL)
        pivot = invert_panel(a_ref[own, own])
        row_ref[...] = mm(pivot, a_ref[own, :])
        row_ref[:, own] = pivot
        col = a_ref[:, own]
        a_ref[:, own] = jnp.zeros_like(col)
        a_ref[...] = a_ref[...] - mm(col, row_ref[...])
        a_ref[own, :] = row_ref[...]


def normal_kernel(vis_ref, obs_ref, keep_ref, one_ref, two_ref, normal_ref, target_ref):
    padded = normal_ref.shape[1]
    directions, rows = vis_ref.shape[1], vis_ref.shape[2]
    stations = padded // directions

    @pl.when(pl.program_id(1) == 0)
    def _():
        normal_ref[...] = jnp.zeros_like(normal_ref)
        target_ref[...] = jnp.zeros_like(target_ref)

    station = lax.broadcasted_iota(jnp.int32, (stations, rows), 0)
    touched = (station == one_ref[...]) | (station == two_ref[...])
    keep = keep_ref[0].astype(jnp.float32)
    vis = vis_ref[0].astype(jnp.float32)
    kept = touched & (keep > 0.0)
    plain = jnp.concatenate(
        [jnp.where(touched, vis[d : d + 1, :], 0.0) for d in range(directions)], axis=0
    ).astype(jnp.bfloat16)
    weighted = jnp.concatenate(
        [jnp.where(kept, vis[d : d + 1, :], 0.0) for d in range(directions)], axis=0
    ).astype(jnp.bfloat16)
    normal_ref[0] += lax.dot_general(
        weighted, plain, (NT, ((), ())), preferred_element_type=jnp.float32
    )
    data = obs_ref[0]
    high = data.astype(jnp.bfloat16).astype(jnp.float32)
    middle = (data - high).astype(jnp.bfloat16).astype(jnp.float32)
    low = data - high - middle
    pieces = jnp.concatenate([high, middle, low, jnp.zeros((5, rows), jnp.float32)], axis=0)
    target_ref[0] += lax.dot_general(
        pieces.astype(jnp.bfloat16), weighted, (NT, ((), ())), preferred_element_type=jnp.float32
    )


def first_kernel(diag_ref, source_ref, down_ref, across_ref, coupling_ref, y_ref, a_ref, row_ref):
    a_ref[...] = diag_ref[...]
    invert_in_place(a_ref, row_ref)
    y_ref[...] = mm(source_ref[...], a_ref[...])
    scaled = a_ref[...] * across_ref[...]
    coupling_ref[...] = scaled * down_ref[...]


def level_kernel(
    diag_ref, lower_ref, above_ref, source_ref,
    xr_ref, xl_ref, up_ref, down_ref, c_ref, y_ref, by_up_ref, by_down_ref, a_ref, row_ref,
):
    a_ref[...] = diag_ref[...]
    invert_in_place(a_ref, row_ref)
    xr_ref[...] = mm(above_ref[...], a_ref[...])
    xl_ref[...] = mm(lower_ref[...], a_ref[...], TN)
    up_ref[...] = mm(xr_ref[...], above_ref[...], NT)
    c_ref[...] = mm(xr_ref[...], lower_ref[...])
    down_ref[...] = mm(xl_ref[...], lower_ref[...])
    y = mm(source_ref[...], a_ref[...])
    y_ref[...] = y
    by_up_ref[...] = mm(y, above_ref[...], NT)
    by_down_ref[...] = mm(y, lower_ref[...])


def last_kernel(diag_ref, source_ref, y_ref, a_ref, row_ref):
    a_ref[...] = diag_ref[...]
    invert_in_place(a_ref, row_ref)
    y_ref[...] = mm(source_ref[...], a_ref[...])


def call(kernel, width, outs, *operands):
    vmem = pl.BlockSpec(memory_space=pltpu.VMEM)
    return pl.pallas_call(
        kernel,
        out_shape=[jax.ShapeDtypeStruct(o, jnp.float32) for o in outs],
        in_specs=[vmem] * len(operands),
        out_specs=[vmem] * len(outs),
        scratch_shapes=[
            pltpu.VMEM((width, width), jnp.float32),
            pltpu.VMEM((PANEL, width), jnp.float32),
        ],
        compiler_params=pltpu.CompilerParams(vmem_limit_bytes=48 << 20),
    )(*operands)


def normals(model_vis, observed, row_keep, station_one, station_two, padded):
    channels, directions, rows = model_vis.shape
    chunk = 1024 if rows % 1024 == 0 else rows
    return pl.pallas_call(
        normal_kernel,
        grid=(channels, rows // chunk),
        out_shape=[
            jax.ShapeDtypeStruct((channels, padded, padded), jnp.float32),
            jax.ShapeDtypeStruct((channels, 8, padded), jnp.float32),
        ],
        in_specs=[
            pl.BlockSpec((1, directions, chunk), lambda f, r: (f, 0, r)),
            pl.BlockSpec((1, 1, chunk), lambda f, r: (f, 0, r)),
            pl.BlockSpec((1, 1, chunk), lambda f, r: (f, 0, r)),
            pl.BlockSpec((1, chunk), lambda f, r: (0, r)),
            pl.BlockSpec((1, chunk), lambda f, r: (0, r)),
        ],
        out_specs=[
            pl.BlockSpec((1, padded, padded), lambda f, r: (f, 0, 0)),
            pl.BlockSpec((1, 8, padded), lambda f, r: (f, 0, 0)),
        ],
        compiler_params=pltpu.CompilerParams(vmem_limit_bytes=48 << 20),
    )(
        model_vis,
        observed.reshape(channels, 1, rows),
        row_keep.reshape(channels, 1, rows),
        station_one.reshape(1, rows),
        station_two.reshape(1, rows),
    )


def move(block, route):
    return lax.ppermute(block, "freq", route)


def body(model_vis, observed, row_keep, station_one, station_two, smoothness):
    channels, directions, _ = model_vis.shape
    assert channels == 2
    devices = lax.axis_size("freq")
    assert devices & (devices - 1) == 0
    position = lax.axis_index("freq")
    stations = smoothness.shape[0] // directions
    slots = -(-stations // 64) * 64
    width = directions * slots
    square, line = (width, width), (8, width)
    smooth = jnp.pad(
        smoothness.reshape(directions, stations), ((0, 0), (0, slots - stations))
    ).reshape(width)

    normal, pieces = normals(model_vis, observed, row_keep, station_one, station_two, width)
    targets = jnp.sum(pieces, axis=1)
    identity = jnp.eye(width, dtype=jnp.float32)

    def diagonal(local):
        channel = position * channels + local
        neighbours = (
            2.0
            - (channel == 0).astype(jnp.float32)
            - (channel == channels * devices - 1).astype(jnp.float32)
        )
        return normal[local] + identity * (ridge_weight + neighbours * smooth)[:, None]

    def as_line(vector):
        return jnp.pad(vector[None, :], ((0, 7), (0, 0)))

    coupling, y0 = call(
        first_kernel, width, (square, line),
        diagonal(0), as_line(targets[0]), smooth[:, None], smooth[None, :],
    )
    back = [(i, i - 1) for i in range(1, devices)]
    from_next = move(coupling, back)
    pulled = y0 * smooth[None, :]
    pulled_next = move(pulled, back)
    diag = diagonal(1) - coupling - from_next
    lower = -jnp.where(position > 0, coupling, 0.0)
    above = -from_next
    source = as_line(targets[1]) + pulled + pulled_next

    levels = (devices - 1).bit_length()
    kept = []
    for level in range(levels):
        stride = 1 << level
        xr, xl, up, down, cross, y, by_up, by_down = call(
            level_kernel, width, (square,) * 5 + (line,) * 3, diag, lower, above, source
        )
        kept.append((xr, xl, y))
        gone = range(stride - 1, devices, 2 * stride)
        rise = [(i, i + stride) for i in gone]
        fall = [(i, i - stride) for i in gone if i >= stride]
        next_gone = range(2 * stride - 1, devices, 4 * stride) if level + 1 < levels else ()
        if fall:
            diag = diag - move(up, rise) - move(down, fall)
            source = source - move(by_up, rise) - move(by_down, fall)
        else:
            diag = diag - move(up, rise)
            source = source - move(by_up, rise)
        if level + 1 < levels:
            lower = -move(cross, [(i, j) for i, j in rise if j in next_gone])
            above = -move(cross, [(i, j) for i, j in fall if j in next_gone])
    (gains,) = call(last_kernel, width, (line,), diag, source)
    for level in reversed(range(levels)):
        stride = 1 << level
        xr, xl, y = kept[level]
        gone = range(stride - 1, devices, 2 * stride)
        from_above = move(gains, [(i + stride, i) for i in gone])
        value = y - mm(from_above, xr)
        falling = [(i - stride, i) for i in gone if i >= stride]
        if falling:
            value = value - mm(move(gains, falling), xl)
        mine = lax.rem(position + 1, 2 * stride) == stride
        gains = jnp.where(mine, value, gains)
    earlier = move(gains, [(i, i + 1) for i in range(devices - 1)])
    scale = jnp.where(smooth > 0, 1.0 / jnp.where(smooth > 0, smooth, 1.0), 0.0)
    first = y0 + mm(earlier + gains, coupling) * scale[None, :]
    both = jnp.stack([first[0], gains[0]])
    return both.reshape(channels, directions, slots)[:, :, :stations].reshape(
        channels, directions * stations
    )


def solution(mesh):
    placed = (P("freq", None, None), P("freq", None), P("freq", None), P(), P(), P())
    return jax.shard_map(
        body, mesh=mesh, in_specs=placed, out_specs=P("freq", None), check_vma=False
    )
```

time: 1930 us -> 685 us (0.35)
  other arithmetic: 1160 us -> 17.9 us
  Pallas kernels: 0 us -> 423 us
  matrix products: 260 us -> 14.7 us
  local copies, waits for them, and re-layouts: 149 us -> 6.88 us
  starting transfers between devices: 116 us -> 52.8 us
  waiting for transfers between devices: 213 us -> 165 us
  between operations: 21.3 us -> 0.94 us
    another operation x143 -> x1, other arithmetic: 855 us -> 0.01 us  [body(): both = jnp.stack([first[0], gains[0]])]
    pallas_call x0 -> x8, Pallas kernels: none -> 423 us  [the longest x7 415 us: call(): pl.pallas_call(kernel, out_shape=[jax.ShapeDtypeStruct(o, jnp.float32) fo...]
    scatter-add x12 -> x0, other arithmetic: 275 us -> none  [the longest x2 48.3 us: normal_system(): jax.ops.segment_sum(outer_terms, pair_two, STATIONS * STATIONS)]
    another operation x140 -> x0, matrix products: 180 us -> none  [the longest x49 68.4 us: solve_with(): return jax.scipy.linalg.solve_triangular(factor, inner, lower=True, trans=1)]
    another operation x135 -> x1, local copies, waits for them, and re-layouts: 84.6 us -> 0.08 us  [body(): smooth[None, :]]
    dot_general x35 -> x10, matrix products: 79.4 us -> 14.7 us  [mm(): lax.dot_general(left, right, (dims, ((), ())), precision=HIGHEST, preferr...]
    ppermute x32 -> x38, starting transfers between devices: 116 us -> 52.8 us  [move(): return lax.ppermute(block, 'freq', route)]
    ppermute x32 -> x38, waiting for transfers between devices: 213 us -> 165 us  [move(): return lax.ppermute(block, 'freq', route)]
  transfers between devices with their start and end apart: 32 -> 38, of which waited for: 10 -> 6; matrix products, arithmetic and copies ran while one was open for 44% -> 2% of each run, Pallas kernels for 0% -> 0%
where the time goes in v1:
time: 685 us; the launch traced here: 681 us
  Pallas kernels  423 us (62%)
  waiting for transfers between devices  165 us (24%)
  starting transfers between devices  52.8 us (8%)
  other arithmetic  17.9 us (3%)
  matrix products  14.7 us (2%)
  local copies, waits for them, and re-layouts  6.88 us (1%)
    pallas_call x7, Pallas kernels, call(): pl.pallas_call(kernel, out_shape=[jax.ShapeDtypeStruct(o, jnp.float32) fo...  415 us
    ppermute x38, waiting for transfers between devices, move(): return lax.ppermute(block, 'freq', route)  165 us
    ppermute x38, starting transfers between devices, move(): return lax.ppermute(block, 'freq', route)  52.8 us
    dot_general x10, matrix products, mm(): lax.dot_general(left, right, (dims, ((), ())), precision=HIGHEST, preferr...  14.7 us
  transfers between devices with their start and end apart: 38, of which 6 were waited for; matrix products, arithmetic and copies ran while one was open for 2% of the time, Pallas kernels for 0%

profile of v1, /device:TPU:8, one launch (start us, length us, event | category | flops | bytes accessed | tf_op | source)
XLA Modules:
  0.0 680.7 jit_solution(16501413302463374146)
XLA Ops:
  2.7 0.9 copy-done.7
  5.0 7.8 %shard_map.64 = (f32[2,512,512]{2,1,0:T(8,128)S(1)}, f32[2,8,512]{2,1,0:T(8,128)S(1)}) custom-call(bf16[2,8,4096]{2,1,0:T(8,128)(2,1)S(1)} %copy-done.7, f32[2,1,4096]{2,1,0:T(1,128)S(1)} %reshape.50.obs_ref, s32[2,1,4096]{2,1,0:T(1,128)S(1)} %reshape.51.keep_ref, s32[1,4096]{1,0:T(1,128)S(1)} %bitcast.30, s32[1,4096]{1,0:T(1,128)S(1)} %bitcast.31), custom_call_target="tpu_custom_call" | custom-call | tf_op jit(solution)/shard_map/pallas_call | solution.py:142
  13.1 51.0 %shard_map.65 = (f32[512,512]{1,0:T(8,128)S(1)}, f32[8,512]{1,0:T(8,128)S(1)}) custom-call(f32[512,512]{1,0:T(8,128)S(1)} %bitcast_add_fusion.1.diag_ref, f32[8,512]{1,0:T(8,128)S(1)} %pad.12.source_ref, f32[512,1]{1,0:T(8,128)S(1)} %reshape.59.down_ref, f32[1,512]{1,0:T(1,128)S(1)} %broadcast_in_dim_reshape.2.across_ref), custom_call_target="tpu_custom_call" | custom-call | tf_op jit(solution)/shard_map/pallas_call | solution.py:126
  64.1 7.2 %collective-permute-start = (f32[512,512]{1,0:T(8,128)S(1)}, f32[512,512]{1,0:T(8,128)}, u32[]{:S(2)}, u32[]{:S(2)}) collective-permute-start(f32[512,512]{1,0:T(8,128)S(1)} %get-tuple-element.48), channel_id=1, source_target_pairs={{1,0},{2,1},{3,2},{4,3},{5,4},{6,5},{7,6},{8,7},{9,8},{10,9},{11,1... | collective-permute-start | bytes 3145736 | tf_op jit(solution)/shard_map/ppermute | solution.py:171
  71.4 7.9 %collective-permute-start.1 = (f32[8,512]{1,0:T(8,128)S(1)}, f32[8,512]{1,0:T(8,128)S(1)}, u32[]{:S(2)}, u32[]{:S(2)}) collective-permute-start(f32[8,512]{1,0:T(8,128)S(1)} %broadcast_multiply_fusion), channel_id=1, source_target_pairs={{1,0},{2,1},{3,2},{4,3},{5,4},{6,5},{7,6},{8,7},{9,8},{10,9},{11,1... | collective-permute-start | bytes 49160 | tf_op jit(solution)/shard_map/ppermute | solution.py:171
  79.2 4.6 collective-permute-done.1
  83.8 3.3 fusion.4
  87.1 62.3 %shard_map.66 = (f32[512,512]{1,0:T(8,128)S(1)}, f32[512,512]{1,0:T(8,128)S(1)}, f32[512,512]{1,0:T(8,128)S(1)}, f32[512,512]{1,0:T(8,128)S(1)}, f32[512,512]{1,...) custom-call(f32[512,512]{1,0:T(8,128)} %get-tuple-element.86.diag_ref, ...), custom_call_target="tpu_custom_call" | custom-call | tf_op jit(solution)/shard_map/pallas_call | solution.py:126
  149.5 4.1 collective-permute-start.4
  154.3 1.9 collective-permute-start.2
  156.2 2.1 collective-permute-start.3
  158.3 1.3 collective-permute-start.6
  160.4 3.7 collective-permute-start.7
  164.1 6.6 collective-permute-done.7
  170.7 1.1 neg.32.lower_ref
  171.8 1.1 neg.33.above_ref
  172.9 1.3 subtract_subtract_fusion.3.diag_ref
  174.2 62.3 %shard_map.67 = (f32[512,512]{1,0:T(8,128)S(1)}, f32[512,512]{1,0:T(8,128)S(1)}, f32[512,512]{1,0:T(8,128)S(1)}, f32[512,512]{1,0:T(8,128)S(1)}, f32[512,512]{1,...) custom-call(f32[512,512]{1,0:T(8,128)} %subtract_subtract_fusion.3.diag_ref, ...), custom_call_target="tpu_custom_call" | custom-call | tf_op jit(solution)/shard_map/pallas_call | solution.py:126
  238.8 0.9 collective-permute-start.9
  241.1 1.1 neg.34.lower_ref
  242.2 1.1 neg.35.above_ref
  243.3 1.4 subtract_subtract_fusion.2.diag_ref
  244.6 62.3 %shard_map.68 = (f32[512,512]{1,0:T(8,128)S(1)}, f32[512,512]{1,0:T(8,128)S(1)}, f32[512,512]{1,0:T(8,128)S(1)}, f32[512,512]{1,0:T(8,128)S(1)}, f32[512,512]{1,...) custom-call(f32[512,512]{1,0:T(8,128)} %subtract_subtract_fusion.2.diag_ref, ...), custom_call_target="tpu_custom_call" | custom-call | tf_op jit(solution)/shard_map/pallas_call | solution.py:126
  309.2 1.1 collective-permute-start.15
  311.7 1.1 neg.36.lower_ref
  312.8 1.1 neg.37.above_ref
  314.0 1.3 subtract_subtract_fusion.1.diag_ref
  315.3 62.3 %shard_map.69 = (f32[512,512]{1,0:T(8,128)S(1)}, f32[512,512]{1,0:T(8,128)S(1)}, f32[512,512]{1,0:T(8,128)S(1)}, f32[512,512]{1,0:T(8,128)S(1)}, f32[512,512]{1,...) custom-call(f32[512,512]{1,0:T(8,128)} %subtract_subtract_fusion.1.diag_ref, ...), custom_call_target="tpu_custom_call" | custom-call | tf_op jit(solution)/shard_map/pallas_call | solution.py:126
  379.9 0.9 collective-permute-start.21
  382.2 1.1 neg.38.lower_ref
  383.3 1.1 neg.39.above_ref
  384.4 1.3 subtract_subtract_fusion.diag_ref
  385.8 63.4 %shard_map.70 = (f32[512,512]{1,0:T(8,128)S(1)}, f32[512,512]{1,0:T(8,128)}, f32[512,512]{1,0:T(8,128)S(1)}, f32[512,512]{1,0:T(8,128)}, f32[512,512]{1,0:T(8,12...) custom-call(f32[512,512]{1,0:T(8,128)} %subtract_subtract_fusion.diag_ref, ...), custom_call_target="tpu_custom_call" | custom-call | tf_op jit(solution)/shard_map/pallas_call | solution.py:126
  449.2 1.0 copy-done.6
  451.9 51.1 %shard_map.71 = f32[8,512]{1,0:T(8,128)S(1)} custom-call(f32[512,512]{1,0:T(8,128)S(1)} %sub.121.diag_ref, f32[8,512]{1,0:T(8,128)S(1)} %sub.122.source_ref), custom_call_target="tpu_custom_call" | custom-call | tf_op jit(solution)/shard_map/pallas_call | solution.py:126
  503.7 1.8 fusion.6
  506.9 1.8 fusion.7
  508.7 1.8 subtract_select_fusion.3
  511.9 1.8 fusion.8
  513.8 1.8 subtract_select_fusion.2
  516.9 1.8 fusion.9
  518.8 1.8 subtract_select_fusion.1
  520.6 1.3 collective-permute-start.35
  521.9 1.3 collective-permute-start.36
  523.2 145.8 %collective-permute-done.35 = f32[8,512]{1,0:T(8,128)S(1)} collective-permute-done((f32[8,512]{1,0:T(8,128)S(1)}, f32[8,512]{1,0:T(8,128)S(1)}, u32[]{:S(2)}, u32[]{:S(2)}) %collective-permute-start.35) | collective-permute-done | bytes 16416 | tf_op jit(solution)/shard_map/ppermute | solution.py:171
  669.6 2.0 collective-permute-done.36
  672.2 1.9 collective-permute-start.37
  674.1 4.9 collective-permute-done.37
  (115 shorter events, 25.4 us)
Async XLA Ops:
  64.1 19.7 %collective-permute-start = (f32[512,512]{1,0:T(8,128)S(1)}, f32[512,512]{1,0:T(8,128)}, u32[]{:S(2)}, u32[]{:S(2)}) collective-permute-start(f32[512,512]{1,0:T(8,128)S(1)} %get-tuple-element.48), channel_id=1, source_target_pairs={{1,0},{2,1},{3,2},{4,3},{5,4},{6,5},{7,6},{8,7},{9,8},{10,9},{11,1... | collective-permute-start | bytes 3145736 | tf_op jit(solution)/shard_map/ppermute | solution.py:171
  71.4 12.5 %collective-permute-start.1 = (f32[8,512]{1,0:T(8,128)S(1)}, f32[8,512]{1,0:T(8,128)S(1)}, u32[]{:S(2)}, u32[]{:S(2)}) collective-permute-start(f32[8,512]{1,0:T(8,128)S(1)} %broadcast_multiply_fusion), channel_id=1, source_target_pairs={{1,0},{2,1},{3,2},{4,3},{5,4},{6,5},{7,6},{8,7},{9,8},{10,9},{11,1... | collective-permute-start | bytes 49160 | tf_op jit(solution)/shard_map/ppermute | solution.py:171
  149.5 21.3 %collective-permute-start.4 = (f32[512,512]{1,0:T(8,128)S(1)}, f32[512,512]{1,0:T(8,128)S(1)}, u32[]{:S(2)}, u32[]{:S(2)}) collective-permute-start(f32[512,512]{1,0:T(8,128)S(1)} %get-tuple-element.52), channel_id=1, source_target_pairs={{0,1},{4,5},{8,9},{12,13},{16,17},{20,21},{24,25},{28,29}} | collective-permute-start | bytes 3145736 | tf_op jit(solution)/shard_map/ppermute | solution.py:171
  153.6 18.2 %collective-permute-start.5 = (f32[512,512]{1,0:T(8,128)S(1)}, f32[512,512]{1,0:T(8,128)S(1)}, u32[]{:S(2)}, u32[]{:S(2)}) collective-permute-start(f32[512,512]{1,0:T(8,128)S(1)} %get-tuple-element.52), channel_id=1, source_target_pairs={{2,1},{6,5},{10,9},{14,13},{18,17},{22,21},{26,25},{30,29}} | collective-permute-start | bytes 3145736 | tf_op jit(solution)/shard_map/ppermute | solution.py:171
  154.3 18.6 %collective-permute-start.2 = (f32[512,512]{1,0:T(8,128)S(1)}, f32[512,512]{1,0:T(8,128)S(1)}, u32[]{:S(2)}, u32[]{:S(2)}) collective-permute-start(f32[512,512]{1,0:T(8,128)S(1)} %get-tuple-element.50), channel_id=1, source_target_pairs={{0,1},{2,3},{4,5},{6,7},{8,9},{10,11},{12,13},{14,15},{16,17},{18,... | collective-permute-start | bytes 3145736 | tf_op jit(solution)/shard_map/ppermute | solution.py:171
  156.2 16.7 %collective-permute-start.3 = (f32[512,512]{1,0:T(8,128)S(1)}, f32[512,512]{1,0:T(8,128)S(1)}, u32[]{:S(2)}, u32[]{:S(2)}) collective-permute-start(f32[512,512]{1,0:T(8,128)S(1)} %get-tuple-element.51), channel_id=1, source_target_pairs={{2,1},{4,3},{6,5},{8,7},{10,9},{12,11},{14,13},{16,15},{18,17},{20... | collective-permute-start | bytes 3145736 | tf_op jit(solution)/shard_map/ppermute | solution.py:171
  158.3 2.1 collective-permute-start.6
  160.4 10.3 %collective-permute-start.7 = (f32[8,512]{1,0:T(8,128)S(1)}, f32[8,512]{1,0:T(8,128)S(1)}, u32[]{:S(2)}, u32[]{:S(2)}) collective-permute-start(f32[8,512]{1,0:T(8,128)S(1)} %get-tuple-element.54), channel_id=1, source_target_pairs={{2,1},{4,3},{6,5},{8,7},{10,9},{12,11},{14,13},{16,15},{18,17},{20... | collective-permute-start | bytes 49160 | tf_op jit(solution)/shard_map/ppermute | solution.py:171
  236.6 6.7 copy-start
  236.6 6.7 copy-start.1
  236.6 4.5 collective-permute-start.10
  237.3 4.9 collective-permute-start.11
  238.0 5.2 collective-permute-start.8
  238.8 4.5 collective-permute-start.9
  239.7 0.7 collective-permute-start.12
  240.4 0.7 collective-permute-start.13
  241.1 2.2 copy-start.12
  307.0 7.0 %copy-start.2 = (f32[512,512]{1,0:T(8,128)}, f32[512,512]{1,0:T(8,128)S(1)}, u32[]{:S(2)}) copy-start(f32[512,512]{1,0:T(8,128)S(1)} %get-tuple-element.80) | copy-start | bytes 3145732
  307.0 7.0 %copy-start.3 = (f32[512,512]{1,0:T(8,128)}, f32[512,512]{1,0:T(8,128)S(1)}, u32[]{:S(2)}) copy-start(f32[512,512]{1,0:T(8,128)S(1)} %get-tuple-element.79) | copy-start | bytes 3145732
  307.0 4.7 collective-permute-start.16
  307.7 5.1 collective-permute-start.17
  308.5 5.5 collective-permute-start.14
  309.2 4.8 collective-permute-start.15
  310.3 0.7 collective-permute-start.18
  311.0 0.7 collective-permute-start.19
  311.7 2.3 copy-start.13
  377.7 6.7 copy-start.4
  377.7 6.7 copy-start.5
  377.7 4.5 collective-permute-start.22
  378.4 4.9 collective-permute-start.23
  379.1 5.3 collective-permute-start.20
  379.9 4.5 collective-permute-start.21
  380.8 0.7 collective-permute-start.24
  381.5 0.7 collective-permute-start.25
  382.2 2.3 copy-start.14
  385.8 65.9 %copy-start.10 = (f32[512,512]{1,0:T(8,128)S(1)}, f32[512,512]{1,0:T(8,128)}, u32[]{:S(2)}) copy-start(f32[512,512]{1,0:T(8,128)} %subtract_subtract_fusion.diag_ref) | copy-start | bytes 3145732
  450.2 1.4 collective-permute-start.26
  451.0 0.7 collective-permute-start.27
  503.0 0.7 collective-permute-start.28
  505.5 1.3 collective-permute-start.29
  506.2 2.5 collective-permute-start.30
  510.6 1.3 collective-permute-start.31
  511.2 2.5 collective-permute-start.32
  515.6 1.3 collective-permute-start.33
  516.3 2.5 collective-permute-start.34
  520.6 148.4 %collective-permute-start.35 = (f32[8,512]{1,0:T(8,128)S(1)}, f32[8,512]{1,0:T(8,128)S(1)}, u32[]{:S(2)}, u32[]{:S(2)}) collective-permute-start(f32[8,512]{1,0:T(8,128)S(1)} %subtract_select_fusion.1), channel_id=1, source_target_pairs={{1,0},{3,2},{5,4},{7,6},{9,8},{11,10},{13,12},{15,14},{17,16},{19,... | collective-permute-start | bytes 49160 | tf_op jit(solution)/shard_map/ppermute | solution.py:171
  521.9 149.7 %collective-permute-start.36 = (f32[8,512]{1,0:T(8,128)S(1)}, f32[8,512]{1,0:T(8,128)S(1)}, u32[]{:S(2)}, u32[]{:S(2)}) collective-permute-start(f32[8,512]{1,0:T(8,128)S(1)} %subtract_select_fusion.1), channel_id=1, source_target_pairs={{1,2},{3,4},{5,6},{7,8},{9,10},{11,12},{13,14},{15,16},{17,18},{19... | collective-permute-start | bytes 49160 | tf_op jit(solution)/shard_map/ppermute | solution.py:171
  672.2 6.9 %collective-permute-start.37 = (f32[8,512]{1,0:T(8,128)S(1)}, f32[8,512]{1,0:T(8,128)S(1)}, u32[]{:S(2)}, u32[]{:S(2)}) collective-permute-start(f32[8,512]{1,0:T(8,128)S(1)} %subtract_select_fusion), channel_id=1, source_target_pairs={{0,1},{1,2},{2,3},{3,4},{4,5},{5,6},{6,7},{7,8},{8,9},{9,10},{10,1... | collective-permute-start | bytes 49160 | tf_op jit(solution)/shard_map/ppermute | solution.py:171
  (5 other events, 5.6 us)

commit v2 on v1

--- a/solution.py
+++ b/solution.py
@@ -8,6 +8,8 @@
 ridge_weight = 1.0
 PANEL = 128
 GROUP = 16
+SUB = 8
+PIVOTS = 4
 HIGHEST = lax.Precision.HIGHEST
 
 
@@ -21,24 +23,62 @@
 TN = ((0,), (0,))
 
 
+def small_inverse(entries):
+    size = len(entries)
+    for m in range(size):
+        inv = 1.0 / entries[m][m]
+        scaled = [inv if j == m else entries[m][j] * inv for j in range(size)]
+        entries = [
+            scaled
+            if i == m
+            else [
+                -(entries[i][m] * inv) if j == m else entries[i][j] - entries[i][m] * scaled[j]
+                for j in range(size)
+            ]
+            for i in range(size)
+        ]
+    return entries
+
+
 def invert_panel(block):
     size = block.shape[0]
-    lane = lax.broadcasted_iota(jnp.int32, (1, size), 1)
-    sub = lax.broadcasted_iota(jnp.int32, (size, 1), 0)
+    strips = size // SUB
+    lane = lax.broadcasted_iota(jnp.int32, (SUB, size), 1)
+    sub = lax.broadcasted_iota(jnp.int32, (SUB, size), 0)
+
+    def spread(value):
+        return jnp.broadcast_to(value, (SUB, size))
 
     def group(_, a):
-        for k in range(GROUP):
-            row = a[k : k + 1, :]
-            col = a[:, k : k + 1]
-            inv = 1.0 / a[k : k + 1, k : k + 1]
-            scaled = jnp.where(lane == k, 1.0, row) * inv
-            factor = jnp.where(sub == k, -1.0, col)
-            rest = jnp.where((lane == k) | (sub == k), 0.0, a)
-            a = rest - factor * scaled
-        a = jnp.concatenate([a[GROUP:, :], a[:GROUP, :]], axis=0)
-        return pltpu.roll(a, size - GROUP, 1)
-
-    return lax.fori_loop(0, size // GROUP, group, block)
+        a = list(a)
+        for k in range(0, GROUP, PIVOTS):
+            home, offset = k // SUB, k % SUB
+            rows = [spread(a[home][offset + i : offset + i + 1, :]) for i in range(PIVOTS)]
+            entries = [
+                [spread(row[:, k + j : k + j + 1]) for j in range(PIVOTS)] for row in rows
+            ]
+            inverse = small_inverse(entries)
+            inside = (lane >= k) & (lane < k + PIVOTS)
+            marked = [
+                jnp.where(inside, jnp.where(lane == k + i, 1.0, 0.0), rows[i])
+                for i in range(PIVOTS)
+            ]
+            scaled = [
+                sum(inverse[i][j] * marked[j] for j in range(PIVOTS)) for i in range(PIVOTS)
+            ]
+            for t in range(strips):
+                value = jnp.where(inside, 0.0, a[t])
+                for i in range(PIVOTS):
+                    value = value - spread(a[t][:, k + i : k + i + 1]) * scaled[i]
+                if t == home:
+                    for i in range(PIVOTS):
+                        value = jnp.where(sub == offset + i, scaled[i], value)
+                a[t] = value
+        shift = GROUP // SUB
+        return tuple(pltpu.roll(a[(t + shift) % strips], size - GROUP, 1) for t in range(strips))
+
+    start = tuple(block[t * SUB : (t + 1) * SUB, :] for t in range(strips))
+    return jnp.concatenate(lax.fori_loop(0, size // GROUP, group, start), axis=0)
 
 
 def invert_in_place(a_ref, row_ref):

time: 685 us -> 552 us (0.81)
  Pallas kernels: 423 us -> 289 us
    pallas_call x7, Pallas kernels: 415 us -> 281 us  [call(): pl.pallas_call(kernel, out_shape=[jax.ShapeDtypeStruct(o, jnp.float32) fo...]
  transfers between devices with their start and end apart: 38 -> 38, of which waited for: 6 -> 6; matrix products, arithmetic and copies ran while one was open for 2% -> 3% of each run, Pallas kernels for 0% -> 0%
where the time goes in v2:
time: 552 us; the launch traced here: 547 us
  Pallas kernels  289 us (52%)
  waiting for transfers between devices  164 us (30%)
  starting transfers between devices  52.9 us (10%)
  other arithmetic  17.9 us (3%)
  matrix products  14.7 us (3%)
  local copies, waits for them, and re-layouts  6.88 us (1%)
    pallas_call x7, Pallas kernels, call(): pl.pallas_call(kernel, out_shape=[jax.ShapeDtypeStruct(o, jnp.float32) fo...  281 us
    ppermute x38, waiting for transfers between devices, move(): return lax.ppermute(block, 'freq', route)  164 us
    ppermute x38, starting transfers between devices, move(): return lax.ppermute(block, 'freq', route)  52.9 us
    dot_general x10, matrix products, mm(): lax.dot_general(left, right, (dims, ((), ())), precision=HIGHEST, preferr...  14.7 us
  transfers between devices with their start and end apart: 38, of which 6 were waited for; matrix products, arithmetic and copies ran while one was open for 3% of the time, Pallas kernels for 0%

profile of v2, /device:TPU:8, one launch (start us, length us, event | category | flops | bytes accessed | tf_op | source)
XLA Modules:
  0.0 546.8 jit_solution(2095449091813657085)
XLA Ops:
  2.7 0.9 copy-done.7
  5.0 7.8 %shard_map.64 = (f32[2,512,512]{2,1,0:T(8,128)S(1)}, f32[2,8,512]{2,1,0:T(8,128)S(1)}) custom-call(bf16[2,8,4096]{2,1,0:T(8,128)(2,1)S(1)} %copy-done.7, f32[2,1,4096]{2,1,0:T(1,128)S(1)} %reshape.50.obs_ref, s32[2,1,4096]{2,1,0:T(1,128)S(1)} %reshape.51.keep_ref, s32[1,4096]{1,0:T(1,128)S(1)} %bitcast.30, s32[1,4096]{1,0:T(1,128)S(1)} %bitcast.31), custom_call_target="tpu_custom_call" | custom-call | tf_op jit(solution)/shard_map/pallas_call | solution.py:182
  13.1 31.9 %shard_map.65 = (f32[512,512]{1,0:T(8,128)S(1)}, f32[8,512]{1,0:T(8,128)S(1)}) custom-call(f32[512,512]{1,0:T(8,128)S(1)} %bitcast_add_fusion.1.diag_ref, f32[8,512]{1,0:T(8,128)S(1)} %pad.12.source_ref, f32[512,1]{1,0:T(8,128)S(1)} %reshape.59.down_ref, f32[1,512]{1,0:T(1,128)S(1)} %broadcast_in_dim_reshape.2.across_ref), custom_call_target="tpu_custom_call" | custom-call | tf_op jit(solution)/shard_map/pallas_call | solution.py:166
  45.0 7.2 %collective-permute-start = (f32[512,512]{1,0:T(8,128)S(1)}, f32[512,512]{1,0:T(8,128)}, u32[]{:S(2)}, u32[]{:S(2)}) collective-permute-start(f32[512,512]{1,0:T(8,128)S(1)} %get-tuple-element.48), channel_id=1, source_target_pairs={{1,0},{2,1},{3,2},{4,3},{5,4},{6,5},{7,6},{8,7},{9,8},{10,9},{11,1... | collective-permute-start | bytes 3145736 | tf_op jit(solution)/shard_map/ppermute | solution.py:211
  52.3 7.7 %collective-permute-start.1 = (f32[8,512]{1,0:T(8,128)S(1)}, f32[8,512]{1,0:T(8,128)S(1)}, u32[]{:S(2)}, u32[]{:S(2)}) collective-permute-start(f32[8,512]{1,0:T(8,128)S(1)} %broadcast_multiply_fusion), channel_id=1, source_target_pairs={{1,0},{2,1},{3,2},{4,3},{5,4},{6,5},{7,6},{8,7},{9,8},{10,9},{11,1... | collective-permute-start | bytes 49160 | tf_op jit(solution)/shard_map/ppermute | solution.py:211
  60.0 4.7 collective-permute-done.1
  64.8 3.3 fusion.4
  68.1 43.5 %shard_map.66 = (f32[512,512]{1,0:T(8,128)S(1)}, f32[512,512]{1,0:T(8,128)S(1)}, f32[512,512]{1,0:T(8,128)S(1)}, f32[512,512]{1,0:T(8,128)S(1)}, f32[512,512]{1,...) custom-call(f32[512,512]{1,0:T(8,128)} %get-tuple-element.86.diag_ref, ...), custom_call_target="tpu_custom_call" | custom-call | tf_op jit(solution)/shard_map/pallas_call | solution.py:166
  111.5 3.7 collective-permute-start.4
  116.0 2.3 collective-permute-start.2
  118.2 2.1 collective-permute-start.3
  120.4 1.3 collective-permute-start.6
  122.5 3.7 collective-permute-start.7
  126.2 6.6 %collective-permute-done.7 = f32[8,512]{1,0:T(8,128)S(1)} collective-permute-done((f32[8,512]{1,0:T(8,128)S(1)}, f32[8,512]{1,0:T(8,128)S(1)}, u32[]{:S(2)}, u32[]{:S(2)}) %collective-permute-start.7) | collective-permute-done | bytes 16416 | tf_op jit(solution)/shard_map/ppermute | solution.py:211
  132.8 1.1 neg.32.lower_ref
  133.9 1.1 neg.33.above_ref
  135.0 1.3 subtract_subtract_fusion.3.diag_ref
  136.3 43.3 %shard_map.67 = (f32[512,512]{1,0:T(8,128)S(1)}, f32[512,512]{1,0:T(8,128)S(1)}, f32[512,512]{1,0:T(8,128)S(1)}, f32[512,512]{1,0:T(8,128)S(1)}, f32[512,512]{1,...) custom-call(f32[512,512]{1,0:T(8,128)} %subtract_subtract_fusion.3.diag_ref, ...), custom_call_target="tpu_custom_call" | custom-call | tf_op jit(solution)/shard_map/pallas_call | solution.py:166
  181.0 0.9 collective-permute-start.8
  184.1 1.1 neg.34.lower_ref
  185.2 1.1 neg.35.above_ref
  186.3 1.4 subtract_subtract_fusion.2.diag_ref
  187.7 43.3 %shard_map.68 = (f32[512,512]{1,0:T(8,128)S(1)}, f32[512,512]{1,0:T(8,128)S(1)}, f32[512,512]{1,0:T(8,128)S(1)}, f32[512,512]{1,0:T(8,128)S(1)}, f32[512,512]{1,...) custom-call(f32[512,512]{1,0:T(8,128)} %subtract_subtract_fusion.2.diag_ref, ...), custom_call_target="tpu_custom_call" | custom-call | tf_op jit(solution)/shard_map/pallas_call | solution.py:166
  232.4 1.1 collective-permute-start.14
  235.7 1.1 neg.36.lower_ref
  236.8 1.1 neg.37.above_ref
  238.0 1.3 subtract_subtract_fusion.1.diag_ref
  239.3 43.3 %shard_map.69 = (f32[512,512]{1,0:T(8,128)S(1)}, f32[512,512]{1,0:T(8,128)S(1)}, f32[512,512]{1,0:T(8,128)S(1)}, f32[512,512]{1,0:T(8,128)S(1)}, f32[512,512]{1,...) custom-call(f32[512,512]{1,0:T(8,128)} %subtract_subtract_fusion.1.diag_ref, ...), custom_call_target="tpu_custom_call" | custom-call | tf_op jit(solution)/shard_map/pallas_call | solution.py:166
  284.0 0.9 collective-permute-start.20
  287.1 1.1 neg.38.lower_ref
  288.2 1.1 neg.39.above_ref
  289.3 1.3 subtract_subtract_fusion.diag_ref
  290.7 44.4 %shard_map.70 = (f32[512,512]{1,0:T(8,128)S(1)}, f32[512,512]{1,0:T(8,128)}, f32[512,512]{1,0:T(8,128)S(1)}, f32[512,512]{1,0:T(8,128)}, f32[512,512]{1,0:T(8,12...) custom-call(f32[512,512]{1,0:T(8,128)} %subtract_subtract_fusion.diag_ref, ...), custom_call_target="tpu_custom_call" | custom-call | tf_op jit(solution)/shard_map/pallas_call | solution.py:166
  335.0 1.0 copy-done.6
  337.9 31.9 %shard_map.71 = f32[8,512]{1,0:T(8,128)S(1)} custom-call(f32[512,512]{1,0:T(8,128)S(1)} %sub.121.diag_ref, f32[8,512]{1,0:T(8,128)S(1)} %sub.122.source_ref), custom_call_target="tpu_custom_call" | custom-call | tf_op jit(solution)/shard_map/pallas_call | solution.py:166
  370.5 1.8 fusion.6
  373.7 1.8 fusion.7
  375.5 1.8 subtract_select_fusion.3
  378.7 1.8 fusion.8
  380.5 1.8 subtract_select_fusion.2
  383.7 1.8 fusion.9
  385.6 1.8 subtract_select_fusion.1
  387.4 1.3 collective-permute-start.35
  388.7 1.3 collective-permute-start.36
  390.0 145.2 %collective-permute-done.35 = f32[8,512]{1,0:T(8,128)S(1)} collective-permute-done((f32[8,512]{1,0:T(8,128)S(1)}, f32[8,512]{1,0:T(8,128)S(1)}, u32[]{:S(2)}, u32[]{:S(2)}) %collective-permute-start.35) | collective-permute-done | bytes 16416 | tf_op jit(solution)/shard_map/ppermute | solution.py:211
  535.8 2.0 collective-permute-done.36
  538.4 1.9 collective-permute-start.37
  540.3 4.9 collective-permute-done.37
  (115 shorter events, 25.6 us)
Async XLA Ops:
  45.0 19.7 %collective-permute-start = (f32[512,512]{1,0:T(8,128)S(1)}, f32[512,512]{1,0:T(8,128)}, u32[]{:S(2)}, u32[]{:S(2)}) collective-permute-start(f32[512,512]{1,0:T(8,128)S(1)} %get-tuple-element.48), channel_id=1, source_target_pairs={{1,0},{2,1},{3,2},{4,3},{5,4},{6,5},{7,6},{8,7},{9,8},{10,9},{11,1... | collective-permute-start | bytes 3145736 | tf_op jit(solution)/shard_map/ppermute | solution.py:211
  52.3 12.5 %collective-permute-start.1 = (f32[8,512]{1,0:T(8,128)S(1)}, f32[8,512]{1,0:T(8,128)S(1)}, u32[]{:S(2)}, u32[]{:S(2)}) collective-permute-start(f32[8,512]{1,0:T(8,128)S(1)} %broadcast_multiply_fusion), channel_id=1, source_target_pairs={{1,0},{2,1},{3,2},{4,3},{5,4},{6,5},{7,6},{8,7},{9,8},{10,9},{11,1... | collective-permute-start | bytes 49160 | tf_op jit(solution)/shard_map/ppermute | solution.py:211
  111.5 21.3 %collective-permute-start.4 = (f32[512,512]{1,0:T(8,128)S(1)}, f32[512,512]{1,0:T(8,128)S(1)}, u32[]{:S(2)}, u32[]{:S(2)}) collective-permute-start(f32[512,512]{1,0:T(8,128)S(1)} %get-tuple-element.52), channel_id=1, source_target_pairs={{0,1},{4,5},{8,9},{12,13},{16,17},{20,21},{24,25},{28,29}} | collective-permute-start | bytes 3145736 | tf_op jit(solution)/shard_map/ppermute | solution.py:211
  115.2 18.6 %collective-permute-start.5 = (f32[512,512]{1,0:T(8,128)S(1)}, f32[512,512]{1,0:T(8,128)S(1)}, u32[]{:S(2)}, u32[]{:S(2)}) collective-permute-start(f32[512,512]{1,0:T(8,128)S(1)} %get-tuple-element.52), channel_id=1, source_target_pairs={{2,1},{6,5},{10,9},{14,13},{18,17},{22,21},{26,25},{30,29}} | collective-permute-start | bytes 3145736 | tf_op jit(solution)/shard_map/ppermute | solution.py:211
  116.0 19.0 %collective-permute-start.2 = (f32[512,512]{1,0:T(8,128)S(1)}, f32[512,512]{1,0:T(8,128)S(1)}, u32[]{:S(2)}, u32[]{:S(2)}) collective-permute-start(f32[512,512]{1,0:T(8,128)S(1)} %get-tuple-element.50), channel_id=1, source_target_pairs={{0,1},{2,3},{4,5},{6,7},{8,9},{10,11},{12,13},{14,15},{16,17},{18,... | collective-permute-start | bytes 3145736 | tf_op jit(solution)/shard_map/ppermute | solution.py:211
  118.2 16.7 %collective-permute-start.3 = (f32[512,512]{1,0:T(8,128)S(1)}, f32[512,512]{1,0:T(8,128)S(1)}, u32[]{:S(2)}, u32[]{:S(2)}) collective-permute-start(f32[512,512]{1,0:T(8,128)S(1)} %get-tuple-element.51), channel_id=1, source_target_pairs={{2,1},{4,3},{6,5},{8,7},{10,9},{12,11},{14,13},{16,15},{18,17},{20... | collective-permute-start | bytes 3145736 | tf_op jit(solution)/shard_map/ppermute | solution.py:211
  120.4 2.1 collective-permute-start.6
  122.5 10.3 %collective-permute-start.7 = (f32[8,512]{1,0:T(8,128)S(1)}, f32[8,512]{1,0:T(8,128)S(1)}, u32[]{:S(2)}, u32[]{:S(2)}) collective-permute-start(f32[8,512]{1,0:T(8,128)S(1)} %get-tuple-element.54), channel_id=1, source_target_pairs={{2,1},{4,3},{6,5},{8,7},{10,9},{12,11},{14,13},{16,15},{18,17},{20... | collective-permute-start | bytes 49160 | tf_op jit(solution)/shard_map/ppermute | solution.py:211
  179.6 6.7 %copy-start = (f32[512,512]{1,0:T(8,128)}, f32[512,512]{1,0:T(8,128)S(1)}, u32[]{:S(2)}) copy-start(f32[512,512]{1,0:T(8,128)S(1)} %get-tuple-element.82) | copy-start | bytes 3145732
  179.6 6.7 %copy-start.1 = (f32[512,512]{1,0:T(8,128)}, f32[512,512]{1,0:T(8,128)S(1)}, u32[]{:S(2)}) copy-start(f32[512,512]{1,0:T(8,128)S(1)} %get-tuple-element.81) | copy-start | bytes 3145732
  179.6 4.5 collective-permute-start.10
  180.3 4.9 collective-permute-start.11
  181.0 5.2 collective-permute-start.8
  182.0 4.3 collective-permute-start.9
  182.7 0.7 collective-permute-start.12
  183.4 0.7 collective-permute-start.13
  184.1 2.2 copy-start.12
  230.9 7.0 %copy-start.2 = (f32[512,512]{1,0:T(8,128)}, f32[512,512]{1,0:T(8,128)S(1)}, u32[]{:S(2)}) copy-start(f32[512,512]{1,0:T(8,128)S(1)} %get-tuple-element.80) | copy-start | bytes 3145732
  230.9 7.0 %copy-start.3 = (f32[512,512]{1,0:T(8,128)}, f32[512,512]{1,0:T(8,128)S(1)}, u32[]{:S(2)}) copy-start(f32[512,512]{1,0:T(8,128)S(1)} %get-tuple-element.79) | copy-start | bytes 3145732
  230.9 4.7 collective-permute-start.16
  231.7 5.1 collective-permute-start.17
  232.4 5.5 %collective-permute-start.14 = (f32[512,512]{1,0:T(8,128)S(1)}, f32[512,512]{1,0:T(8,128)S(1)}, u32[]{:S(2)}, u32[]{:S(2)}) collective-permute-start(f32[512,512]{1,0:T(8,128)S(1)} %get-tuple-element.62), channel_id=1, source_target_pairs={{3,7},{11,15},{19,23},{27,31}} | collective-permute-start | bytes 3145736 | tf_op jit(solution)/shard_map/ppermute | solution.py:211
  233.6 4.4 collective-permute-start.15
  234.3 0.7 collective-permute-start.18
  235.0 0.7 collective-permute-start.19
  235.7 2.3 copy-start.13
  282.6 6.7 %copy-start.4 = (f32[512,512]{1,0:T(8,128)}, f32[512,512]{1,0:T(8,128)S(1)}, u32[]{:S(2)}) copy-start(f32[512,512]{1,0:T(8,128)S(1)} %get-tuple-element.78) | copy-start | bytes 3145732
  282.6 6.7 %copy-start.5 = (f32[512,512]{1,0:T(8,128)}, f32[512,512]{1,0:T(8,128)S(1)}, u32[]{:S(2)}) copy-start(f32[512,512]{1,0:T(8,128)S(1)} %get-tuple-element.77) | copy-start | bytes 3145732
  282.6 4.5 collective-permute-start.22
  283.3 4.9 collective-permute-start.23
  284.0 5.3 collective-permute-start.20
  285.0 4.4 collective-permute-start.21
  285.7 0.7 collective-permute-start.24
  286.4 0.7 collective-permute-start.25
  287.1 2.3 copy-start.14
  290.7 47.1 %copy-start.10 = (f32[512,512]{1,0:T(8,128)S(1)}, f32[512,512]{1,0:T(8,128)}, u32[]{:S(2)}) copy-start(f32[512,512]{1,0:T(8,128)} %subtract_subtract_fusion.diag_ref) | copy-start | bytes 3145732
  336.1 1.6 collective-permute-start.26
  336.8 0.9 collective-permute-start.27
  369.8 0.7 collective-permute-start.28
  372.3 1.3 collective-permute-start.29
  373.0 2.5 collective-permute-start.30
  377.4 1.3 collective-permute-start.31
  378.0 2.5 collective-permute-start.32
  382.4 1.3 collective-permute-start.33
  383.0 2.5 collective-permute-start.34
  387.4 147.8 %collective-permute-start.35 = (f32[8,512]{1,0:T(8,128)S(1)}, f32[8,512]{1,0:T(8,128)S(1)}, u32[]{:S(2)}, u32[]{:S(2)}) collective-permute-start(f32[8,512]{1,0:T(8,128)S(1)} %subtract_select_fusion.1), channel_id=1, source_target_pairs={{1,0},{3,2},{5,4},{7,6},{9,8},{11,10},{13,12},{15,14},{17,16},{19,... | collective-permute-start | bytes 49160 | tf_op jit(solution)/shard_map/ppermute | solution.py:211
  388.7 149.1 %collective-permute-start.36 = (f32[8,512]{1,0:T(8,128)S(1)}, f32[8,512]{1,0:T(8,128)S(1)}, u32[]{:S(2)}, u32[]{:S(2)}) collective-permute-start(f32[8,512]{1,0:T(8,128)S(1)} %subtract_select_fusion.1), channel_id=1, source_target_pairs={{1,2},{3,4},{5,6},{7,8},{9,10},{11,12},{13,14},{15,16},{17,18},{19... | collective-permute-start | bytes 49160 | tf_op jit(solution)/shard_map/ppermute | solution.py:211
  538.4 6.9 %collective-permute-start.37 = (f32[8,512]{1,0:T(8,128)S(1)}, f32[8,512]{1,0:T(8,128)S(1)}, u32[]{:S(2)}, u32[]{:S(2)}) collective-permute-start(f32[8,512]{1,0:T(8,128)S(1)} %subtract_select_fusion), channel_id=1, source_target_pairs={{0,1},{1,2},{2,3},{3,4},{4,5},{5,6},{6,7},{7,8},{8,9},{9,10},{10,1... | collective-permute-start | bytes 49160 | tf_op jit(solution)/shard_map/ppermute | solution.py:211
  (5 other events, 5.6 us)
